TPU v7x, 128 devices: a whole 4x4x4 slice. The times are simulated.
128 devices in a mesh: lat: 8 (over x, core), lon: 16 (over y, z).
Axes of the slice: x: 4, y: 4, z: 4, core: 2. Of those that a mesh axis runs over, the one named last changes fastest.
Arguments:
- adjoint_in: float32 [16, 72, 64, 2048], P(None, None, 'lat', 'lon'), may hold values from -6 to 6
- horiz_frac: float32 [2, 4, 72, 64, 2048], P(None, None, None, 'lat', 'lon'), may hold values from 0 to 0.22
- vert_frac: float32 [2, 2, 72, 64, 2048], P(None, None, None, 'lat', 'lon'), may hold values from 0 to 0.4
- polar_shift: int32 [2, 4], replicated, may hold values from 1 to 4096
- polar_frac: float32 [2, 4], replicated, may hold values from 0 to 1
- sound_forcing: float32 [128, 128, 1152], P(('lat', 'lon')), may hold values from -6 to 6
- sound_col: int32 [128, 128, 16], P(('lat', 'lon')), may hold values from 0 to 1023
- sound_count: int32 [128, 128], P(('lat', 'lon')), may hold values from 0 to 16, as said below
Outputs:
- adjoint_out: float32 [16, 72, 64, 2048], P(None, None, 'lat', 'lon')
Inputs may be any that keep to these rules, and one draw needn't show every extreme that they name: `sound_count`: in each draw some owning device has all 16 slots filled from every sender.
All inputs are finite; a program needn't handle non-finite values.
Results may differ from a plain program's by a relative error of at most 0.0003.
Values sent between devices are 32-bit elements; how exact they have to be, the bound alone decides.
A program may use at most 128 MiB of HBM per device.

v0:
```python
import functools

import jax
import jax.numpy as jnp
from jax import lax
from jax.experimental import pallas as pl
from jax.experimental.pallas import tpu as pltpu
from jax.sharding import PartitionSpec as P

MESH = pl.DeviceIdType.MESH
NPOLE = 2
STEPS = 2
GROUP = 4
PITCH = 16
BLOCK = 8


def log_of(value):
    shifted = value - 1.0
    z = shifted / (2.0 + shifted)
    square = z * z
    total = jnp.full_like(z, 1.0 / 17.0)
    for odd in (15, 13, 11, 9, 7, 5, 3, 1):
        total = total * square + 1.0 / odd
    return 2.0 * z * total


def halves(value):
    high = value.astype(jnp.bfloat16)
    return high, (value - high.astype(jnp.float32)).astype(jnp.bfloat16)


def kernel(
    sizes,
    shift_ref,
    frac_ref,
    adjoint_hbm,
    horiz_hbm,
    vert_hbm,
    sound_hbm,
    col_ref,
    count_ref,
    out_hbm,
    extra_hbm,
    field,
    horiz,
    vert,
    padded,
    owned,
    parts,
    turned,
    first_recv,
    second_send,
    second_recv,
    row_send,
    row_recv,
    col_send,
    col_recv,
    pole_send,
    pole_recv,
    pole_part,
    extra_row_send,
    extra_row_recv,
    extra_col_send,
    extra_col_recv,
    extra_pole_send,
    extra_pole_recv,
    extra_pole_part,
    pole_matrix,
    load_sem,
    out_sem,
    first_send_sem,
    first_recv_sem,
    second_send_sem,
    second_recv_sem,
    row_send_sem,
    row_recv_sem,
    col_send_sem,
    col_recv_sem,
    pole_send_sem,
    pole_recv_sem,
):
    tracers, levels, lats, lons, n_lat, n_lon, slots = sizes
    groups = tracers // GROUP
    blocks = levels // BLOCK
    senders = n_lat * n_lon
    chunks = slots * levels // lons
    lat = lax.axis_index("lat")
    lon = lax.axis_index("lon")
    north = lax.rem(lat + 1, n_lat)
    south = lax.rem(lat + n_lat - 1, n_lat)
    east = lax.rem(lon + 1, n_lon)
    west = lax.rem(lon + n_lon - 1, n_lon)
    at_top = lat == 0
    is_polar = at_top | (lat == n_lat - 1)
    pole_row = jnp.where(at_top, 0, lats - NPOLE)
    first_pole = jnp.where(at_top, 0, NPOLE)

    lane = lax.broadcasted_iota(jnp.int32, (lats, lons), 1)
    sub = lax.broadcasted_iota(jnp.int32, (lats, lons), 0)

    volume = tracers * levels * lats
    load_vert = pltpu.make_async_copy(vert_hbm, vert, load_sem.at[0])
    load_field = pltpu.make_async_copy(adjoint_hbm, field.at[pl.ds(0, volume)], load_sem.at[1])
    load_horiz = pltpu.make_async_copy(horiz_hbm, horiz, load_sem.at[2])
    load_own = pltpu.make_async_copy(
        sound_hbm.at[pl.ds(lat * n_lon, n_lon)], first_recv.at[lat], load_sem.at[3]
    )
    load_vert.start()
    load_field.start()
    load_horiz.start()
    load_own.start()

    barrier = pltpu.get_barrier_semaphore()
    for d in range(1, n_lat):
        pl.semaphore_signal(
            barrier, inc=1, device_id=(lax.rem(lat + d, n_lat), lon), device_id_type=MESH
        )
    for d in range(1, n_lon):
        pl.semaphore_signal(
            barrier, inc=1, device_id=(lat, lax.rem(lon + d, n_lon)), device_id_type=MESH
        )

    def courant(step, p):
        return shift_ref[step, first_pole + p].astype(jnp.float32) + frac_ref[step, first_pole + p]

    def log_retain(step, p, shape):
        c = jnp.full(shape, courant(step, p), jnp.float32)
        return log_of(c / (1.0 + c))

    @pl.when(is_polar)
    def _():
        j = lax.broadcasted_iota(jnp.int32, (lons, lons), 0)
        i = lax.broadcasted_iota(jnp.int32, (lons, lons), 1)
        distance = (j - i).astype(jnp.float32)
        for step in range(STEPS):
            for p in range(NPOLE):
                power = jnp.exp(jnp.maximum(distance, 0.0) * log_retain(step, p, (lons, lons)))
                weight = 1.0 / (1.0 + jnp.full((lons, lons), courant(step, p), jnp.float32))
                matrix = jnp.where(distance >= 0.0, power, 0.0) * weight
                high, low = halves(matrix)
                pole_matrix[step, p, 0:lons, :] = high
                pole_matrix[step, p, lons : 2 * lons, :] = high
                pole_matrix[step, p, 2 * lons : 3 * lons, :] = low

    counts = jnp.broadcast_to(count_ref[...], (senders, senders)).T
    slot = lax.broadcasted_iota(jnp.int32, (senders, slots), 1)
    columns = jnp.where(slot < counts[:, :slots], col_ref[...], -1)
    for j in range(slots):
        spread = jnp.broadcast_to(columns[:, j : j + 1], (senders, lons))
        for a in range(n_lat):
            owned[pl.ds(j * senders + a, n_lon, stride=n_lat), :] = spread[
                a * n_lon : (a + 1) * n_lon
            ]

    pl.semaphore_wait(barrier, n_lat + n_lon - 2)

    def first_copy(d):
        target = lax.rem(lat + d, n_lat)
        return pltpu.make_async_remote_copy(
            src_ref=sound_hbm.at[pl.ds(target * n_lon, n_lon)],
            dst_ref=first_recv.at[lat],
            send_sem=first_send_sem.at[d],
            recv_sem=first_recv_sem.at[lat],
            device_id=(target, lon),
            device_id_type=MESH,
        )

    def first_arrival(d):
        source = lax.rem(lat + d, n_lat)
        return pltpu.make_async_remote_copy(
            src_ref=first_recv.at[source],
            dst_ref=first_recv.at[source],
            send_sem=first_send_sem.at[d],
            recv_sem=first_recv_sem.at[source],
            device_id=(source, lon),
            device_id_type=MESH,
        )

    share = chunks * n_lat

    def second_copy(d):
        target = lax.rem(lon + d, n_lon)
        return pltpu.make_async_remote_copy(
            src_ref=second_send.at[pl.ds(target * share, share)],
            dst_ref=second_recv.at[pl.ds(lon * share, share)],
            send_sem=second_send_sem.at[d],
            recv_sem=second_recv_sem.at[lon],
            device_id=(lat, target),
            device_id_type=MESH,
        )

    def second_arrival(d):
        source = lax.rem(lon + d, n_lon)
        here = second_recv.at[pl.ds(source * share, share)]
        return pltpu.make_async_remote_copy(
            src_ref=here,
            dst_ref=here,
            send_sem=second_send_sem.at[d],
            recv_sem=second_recv_sem.at[source],
            device_id=(lat, source),
            device_id_type=MESH,
        )

    second_own = pltpu.make_async_copy(
        second_send.at[pl.ds(lon * share, share)],
        second_recv.at[pl.ds(lon * share, share)],
        second_recv_sem.at[lon],
    )

    for d in range(1, n_lat):
        first_copy(d).start()

    def forward():
        load_own.wait()
        for d in range(1, n_lat):
            first_arrival(d).wait_recv()
        for a in range(n_lat):
            for half in range(n_lon // 8):
                for i in range(chunks):
                    second_send[pl.ds((half * 8 * chunks + i) * n_lat + a, 8, stride=share), :] = (
                        first_recv[a, half * 8 : half * 8 + 8, i * lons : (i + 1) * lons]
                    )
        for d in range(1, n_lon):
            second_copy(d).start()
        second_own.start()

    extra_base = tracers * levels * lats

    def collect():
        second_own.wait()
        for d in range(1, n_lon):
            second_arrival(d).wait_recv()
        for i in range(chunks):
            rows = [
                second_recv[(b * chunks + i) * n_lat : (b * chunks + i + 1) * n_lat, :]
                for b in range(n_lon)
            ]
            turned[i * lons : (i + 1) * lons, :] = jnp.concatenate(rows, axis=0).T
        gap = jnp.zeros((8, senders), jnp.float32)
        for j in range(slots):
            piece = turned[j * levels : (j + 1) * levels, :]
            high = piece.astype(jnp.bfloat16).astype(jnp.float32)
            rest = piece - high
            middle = rest.astype(jnp.bfloat16).astype(jnp.float32)
            low = rest - middle
            stacked = jnp.concatenate([high, gap, middle, gap, low, gap], axis=0)
            parts[:, j * senders : (j + 1) * senders] = stacked.astype(jnp.bfloat16)
        span = levels + 8

        def place(pair, carry):
            here = lax.broadcasted_iota(jnp.int32, (slots * senders, lons), 1) + pair * (2 * lons)
            cols = owned[...]
            hot = jnp.concatenate(
                [
                    jnp.where(cols == here, 1.0, 0.0).astype(jnp.bfloat16),
                    jnp.where(cols == here + lons, 1.0, 0.0).astype(jnp.bfloat16),
                ],
                axis=1,
            )
            got = jnp.dot(parts[...], hot, preferred_element_type=jnp.float32)
            total = got[:levels] + got[span : span + levels] + got[2 * span : 2 * span + levels]
            field[pl.ds(extra_base + 2 * pair, levels, stride=lats), :] = total[:, :lons]
            field[pl.ds(extra_base + 2 * pair + 1, levels, stride=lats), :] = total[:, lons:]
            return carry

        lax.fori_loop(0, lats // 2, place, 0)

    pair_index = ((lane + 1) >> 1) & (lons // 2 - 1)
    global_row = lat * lats + sub
    polar_mask = (global_row < NPOLE) | (global_row >= n_lat * lats - NPOLE)
    zero = jnp.zeros((lats, lons), jnp.float32)

    class Part:
        def __init__(self, first, count, index, buffers):
            self.first, self.count, self.index = first, count, index
            self.extra = index == groups if isinstance(index, int) else False
            (
                self.row_send,
                self.row_recv,
                self.col_send,
                self.col_recv,
                self.pole_send,
                self.pole_recv,
                self.pole_part,
            ) = buffers

        def base(self, t, level):
            return ((self.first + t) * levels + level) * PITCH + 8

        def tile(self, t, level):
            return pl.ds(pl.multiple_of(((self.first + t) * levels + level) * lats, lats), lats)

        def vertical(self, step):
            count = self.count

            def block(lb, carry):
                first = lb * BLOCK
                before = jnp.maximum(first - 1, 0)
                down_tiles = [field[self.tile(t, before), :] for t in range(count)]
                here_tiles = [field[self.tile(t, first), :] for t in range(count)]
                packed = zero
                for dl in range(BLOCK):
                    level = first + dl
                    after = jnp.minimum(level + 1, levels - 1)
                    up = vert[step, 0, level]
                    down = vert[step, 1, level]
                    keep = 1.0 - up - down
                    for t in range(count):
                        up_tile = field[self.tile(t, after), :]
                        mixed = keep * here_tiles[t] + up * up_tile + down * down_tiles[t]
                        start = pl.multiple_of(self.base(t, level), 8)
                        padded[pl.ds(start, lats), :] = mixed
                        k = dl * count + t
                        turn = mixed if k == 0 else pltpu.roll(mixed, 2 * k, 1)
                        packed = jnp.where(pair_index == k, turn, packed)
                        down_tiles[t] = here_tiles[t]
                        here_tiles[t] = up_tile
                self.col_send(step)[lb] = packed
                for t in range(count):
                    start = self.base(t, first)
                    to = pl.multiple_of(t * levels + first, 8)
                    self.row_send(step, 0)[pl.ds(to, BLOCK), :] = padded[
                        pl.ds(start, BLOCK, stride=PITCH), :
                    ]
                    self.row_send(step, 1)[pl.ds(to, BLOCK), :] = padded[
                        pl.ds(start + lats - 1, BLOCK, stride=PITCH), :
                    ]
                return carry

            lax.fori_loop(0, blocks, block, 0)

        def row_copy(self, step, side):
            return pltpu.make_async_remote_copy(
                src_ref=self.row_send(step, side),
                dst_ref=self.row_recv(step, side),
                send_sem=row_send_sem.at[step, side, self.index],
                recv_sem=row_recv_sem.at[step, side, self.index],
                device_id=(south, lon) if side == 0 else (north, lon),
                device_id_type=MESH,
            )

        def col_copy(self, step, side):
            return pltpu.make_async_remote_copy(
                src_ref=self.col_send(step),
                dst_ref=self.col_recv(step, side),
                send_sem=col_send_sem.at[step, side, self.index],
                recv_sem=col_recv_sem.at[step, side, self.index],
                device_id=(lat, west) if side == 0 else (lat, east),
                device_id_type=MESH,
            )

        def pole_copy(self, step, d):
            return pltpu.make_async_remote_copy(
                src_ref=self.pole_send(step),
                dst_ref=self.pole_recv(step).at[n_lon - d],
                send_sem=pole_send_sem.at[step, self.index, d],
                recv_sem=pole_recv_sem.at[step, self.index, n_lon - d],
                device_id=(lat, lax.rem(lon + d, n_lon)),
                device_id_type=MESH,
            )

        def release(self, step):
            for side in range(2):
                self.row_copy(step, side).start()
                self.col_copy(step, side).start()

        def receive(self, step):
            for side in range(2):
                self.row_copy(step, side).wait_recv()
                self.col_copy(step, side).wait_recv()

        def pole_local(self, step):
            count = self.count

            @pl.when(is_polar)
            def _():
                packed = zero
                for p in range(NPOLE):
                    start = self.base(0, 0) + pole_row + p
                    rows = padded[pl.ds(start, count * levels, stride=PITCH), :]
                    high, low = halves(rows)
                    solved = jnp.dot(
                        jnp.concatenate([high, low, high], axis=1),
                        pole_matrix[step, p],
                        preferred_element_type=jnp.float32,
                    )
                    self.pole_part(step)[p] = solved
                    for q in range(count * blocks):
                        tile = solved[q * 8 : q * 8 + 8]
                        at = p * count * blocks + q
                        turn = tile if at == 0 else pltpu.roll(tile, at, 1)
                        packed = jnp.where(lane == at, turn, packed)
                self.pole_send(step)[...] = packed
                for d in range(1, n_lon):
                    self.pole_copy(step, d).start()

        def pole_finish(self, step):
            count = self.count

            @pl.when(is_polar)
            def _():
                for d in range(1, n_lon):
                    self.pole_copy(step, d).wait_recv()
                logs = [log_retain(step, p, (lats, lons)) for p in range(NPOLE)]
                log = jnp.where(lane < count * blocks, logs[0], logs[1])
                inflow = self.pole_send(step)[...] * jnp.exp((float(lons) * (n_lon - 1)) * log)
                for d in range(1, n_lon):
                    inflow = inflow + self.pole_recv(step)[d] * jnp.exp(
                        (float(lons) * (d - 1)) * log
                    )
                inflow = inflow / (1.0 - jnp.exp(float(lons * n_lon) * log))
                for p in range(NPOLE):
                    carried = jnp.exp((lons - lane).astype(jnp.float32) * logs[p])
                    for q in range(count * blocks):
                        at = p * count * blocks + q
                        start = self.base(0, q * BLOCK) + pole_row + p
                        spread = jnp.broadcast_to(inflow[:, at : at + 1], (lats, lons))
                        padded[pl.ds(start, BLOCK, stride=PITCH), :] = (
                            self.pole_part(step)[p, q * 8 : q * 8 + 8, :] + carried * spread
                        )

        def horizontal(self, step):
            count = self.count

            def block(lb, carry):
                first = lb * BLOCK
                halo = jnp.where(
                    (lane & 1) == 0,
                    self.col_recv(step, 0)[lb],
                    pltpu.roll(self.col_recv(step, 1)[lb], 2, 1),
                )
                for t in range(count):
                    start = self.base(t, first)
                    at = pl.multiple_of(t * levels + first, 8)
                    padded[pl.ds(start + lats, BLOCK, stride=PITCH), :] = self.row_recv(step, 0)[
                        pl.ds(at, BLOCK), :
                    ]
                    padded[pl.ds(start - 1, BLOCK, stride=PITCH), :] = self.row_recv(step, 1)[
                        pl.ds(at, BLOCK), :
                    ]
                for dl in range(BLOCK):
                    level = first + dl
                    e = jnp.where(polar_mask, zero, horiz[step, 0, level])
                    w = jnp.where(polar_mask, zero, horiz[step, 1, level])
                    n = jnp.where(global_row == n_lat * lats - 1, zero, horiz[step, 2, level])
                    s = jnp.where(global_row == 0, zero, horiz[step, 3, level])
                    keep = 1.0 - e - w - n - s
                    edge = jnp.where(lane == lons - 1, e, jnp.where(lane == 0, w, zero))
                    e = jnp.where(lane == lons - 1, zero, e)
                    w = jnp.where(lane == 0, zero, w)
                    for t in range(count):
                        start = pl.multiple_of(self.base(t, level), 8)
                        here = padded[pl.ds(start, lats), :]
                        k = dl * count + t
                        field[self.tile(t, level), :] = (
                            keep * here
                            + e * pltpu.roll(here, lons - 1, 1)
                            + w * pltpu.roll(here, 1, 1)
                            + edge * pltpu.roll(halo, lons - 1 - 2 * k, 1)
                            + n * padded[pl.ds(start + 1, lats), :]
                            + s * padded[pl.ds(start - 1, lats), :]
                        )
                return carry

            lax.fori_loop(0, blocks, block, 0)

        def begin(self, step):
            self.vertical(step)
            self.release(step)
            self.pole_local(step)

        def end(self, step):
            self.receive(step)
            self.pole_finish(step)
            self.horizontal(step)

        def drain(self):
            for step in range(STEPS):
                for side in range(2):
                    self.row_copy(step, side).wait_send()
                    self.col_copy(step, side).wait_send()

                @pl.when(is_polar)
                def _():
                    for d in range(1, n_lon):
                        self.pole_copy(step, d).wait_send()

    def main(g):
        return Part(
            g * GROUP,
            GROUP,
            g,
            (
                lambda step, side: row_send.at[step, side, g],
                lambda step, side: row_recv.at[step, side, g],
                lambda step: col_send.at[step, g],
                lambda step, side: col_recv.at[step, side, g],
                lambda step: pole_send.at[step, g],
                lambda step: pole_recv.at[step, g],
                lambda step: pole_part.at[g],
            ),
        )

    extra = Part(
        tracers,
        1,
        groups,
        (
            lambda step, side: extra_row_send.at[step, side],
            lambda step, side: extra_row_recv.at[step, side],
            lambda step: extra_col_send.at[step],
            lambda step, side: extra_col_recv.at[step, side],
            lambda step: extra_pole_send.at[step],
            lambda step: extra_pole_recv.at[step],
            lambda step: extra_pole_part,
        ),
    )

    def over(lo, hi, body):
        def turn(g, carry):
            body(g)
            return carry

        lax.fori_loop(lo, hi, turn, 0)

    slab = GROUP * levels * lats

    def out_copy(g):
        rows = pl.ds(pl.multiple_of(g * slab, slab), slab)
        return pltpu.make_async_copy(field.at[rows], out_hbm.at[rows], out_sem.at[g])

    def middle(g):
        part = main(g)
        part.end(1)
        part.begin(0)

    def last(g):
        main(g).end(0)
        out_copy(g).start()

    load_vert.wait()
    load_field.wait()
    over(0, groups, lambda g: main(g).begin(1))
    forward()
    load_horiz.wait()
    over(0, groups, middle)
    collect()
    extra.begin(1)
    over(0, 1, last)
    extra.end(1)
    extra.begin(0)
    over(1, groups, last)
    extra.end(0)
    extra_copy = pltpu.make_async_copy(
        field.at[pl.ds(extra_base, levels * lats)], extra_hbm, out_sem.at[groups]
    )
    extra_copy.start()

    for d in range(1, n_lat):
        first_copy(d).wait_send()
    for d in range(1, n_lon):
        second_copy(d).wait_send()
    over(0, groups, lambda g: main(g).drain())
    extra.drain()
    over(0, groups, lambda g: out_copy(g).wait())
    extra_copy.wait()


def transport(mesh_shape, adjoint_in, horiz_frac, vert_frac, shift, frac, sound, cols, counts):
    tracers, levels, lats, lons = adjoint_in.shape
    n_lat, n_lon = mesh_shape
    senders, slots = cols.shape
    groups = tracers // GROUP
    blocks = levels // BLOCK
    per_group = GROUP * levels
    features = sound.shape[1]
    f32 = jnp.float32
    any_spec = pl.BlockSpec(memory_space=pl.ANY)
    vmem = pl.BlockSpec(memory_space=pltpu.VMEM)
    smem = pl.BlockSpec(memory_space=pltpu.SMEM)
    dma = pltpu.SemaphoreType.DMA
    rows = tracers * levels * lats
    out, extra = pl.pallas_call(
        functools.partial(kernel, (tracers, levels, lats, lons, n_lat, n_lon, slots)),
        out_shape=(
            jax.ShapeDtypeStruct((rows, lons), f32),
            jax.ShapeDtypeStruct((levels * lats, lons), f32),
        ),
        in_specs=[smem, smem, any_spec, any_spec, any_spec, any_spec, vmem, vmem],
        out_specs=(any_spec, any_spec),
        scratch_shapes=[
            pltpu.VMEM((rows + levels * lats, lons), f32),
            pltpu.VMEM(horiz_frac.shape, f32),
            pltpu.VMEM(vert_frac.shape, f32),
            pltpu.VMEM(((tracers + 1) * levels * PITCH + 32, lons), f32),
            pltpu.VMEM((slots * senders, lons), jnp.int32),
            pltpu.VMEM((3 * (levels + 8), slots * senders), jnp.bfloat16),
            pltpu.VMEM((features, senders), f32),
            pltpu.VMEM((n_lat, n_lon, features), f32),
            pltpu.VMEM((senders * features // lons, lons), f32),
            pltpu.VMEM((senders * features // lons, lons), f32),
            pltpu.VMEM((STEPS, 2, groups, per_group, lons), f32),
            pltpu.VMEM((STEPS, 2, groups, per_group, lons), f32),
            pltpu.VMEM((STEPS, groups, blocks, lats, lons), f32),
            pltpu.VMEM((STEPS, 2, groups, blocks, lats, lons), f32),
            pltpu.VMEM((STEPS, groups, lats, lons), f32),
            pltpu.VMEM((STEPS, groups, n_lon, lats, lons), f32),
            pltpu.VMEM((groups, NPOLE, per_group, lons), f32),
            pltpu.VMEM((STEPS, 2, levels, lons), f32),
            pltpu.VMEM((STEPS, 2, levels, lons), f32),
            pltpu.VMEM((STEPS, blocks, lats, lons), f32),
            pltpu.VMEM((STEPS, 2, blocks, lats, lons), f32),
            pltpu.VMEM((STEPS, lats, lons), f32),
            pltpu.VMEM((STEPS, n_lon, lats, lons), f32),
            pltpu.VMEM((NPOLE, levels, lons), f32),
            pltpu.VMEM((STEPS, NPOLE, 3 * lons, lons), jnp.bfloat16),
            dma((4,)),
            dma((groups + 1,)),
            dma((n_lat,)),
            dma((n_lat,)),
            dma((n_lon,)),
            dma((n_lon,)),
            dma((STEPS, 2, groups + 1)),
            dma((STEPS, 2, groups + 1)),
            dma((STEPS, 2, groups + 1)),
            dma((STEPS, 2, groups + 1)),
            dma((STEPS, groups + 1, n_lon)),
            dma((STEPS, groups + 1, n_lon)),
        ],
        compiler_params=pltpu.CompilerParams(
            collective_id=0, has_side_effects=True, vmem_limit_bytes=60 * 1024 * 1024
        ),
    )(shift, frac, adjoint_in.reshape(rows, lons), horiz_frac, vert_frac, sound, cols, counts)
    return out.reshape(adjoint_in.shape) + extra.reshape(levels, lats, lons)[None]


def solution(mesh):
    mesh_shape = (mesh.shape["lat"], mesh.shape["lon"])

    def on_device(
        adjoint_in,
        horiz_frac,
        vert_frac,
        polar_shift,
        polar_frac,
        sound_forcing,
        sound_col,
        sound_count,
    ):
        return transport(
            mesh_shape,
            adjoint_in,
            horiz_frac,
            vert_frac,
            polar_shift,
            polar_frac,
            sound_forcing[0],
            sound_col[0],
            sound_count,
        )

    return jax.shard_map(
        on_device,
        mesh=mesh,
        in_specs=(
            P(None, None, "lat", "lon"),
            P(None, None, None, "lat", "lon"),
            P(None, None, None, "lat", "lon"),
            P(),
            P(),
            P(("lat", "lon"), None, None),
            P(("lat", "lon"), None, None),
            P(("lat", "lon"), None),
        ),
        out_specs=P(None, None, "lat", "lon"),
        check_vma=False,
    )
```

profile of v0, /device:TPU:0, one launch (start us, length us, event | category | flops | bytes accessed | tf_op | source)
XLA Modules:
  0.0 62.0 jit_solution(13943026394984166110)
XLA Ops:
  0.0 1.4 %copy.9 = s32[1,128,16]{2,1,0:T(8,128)} copy(s32[1,128,16]{1,2,0:T(8,128)} %param.14) | data formatting | bytes 16384 | tf_op args[6]
  1.4 55.6 %shard_map.82 = (f32[9216,128]{1,0:T(8,128)}, f32[576,128]{1,0:T(8,128)}) custom-call(s32[2,4]{1,0:T(2,128)} %shift_ref.1, f32[2,4]{1,0:T(2,128)} %frac_ref.1, f32[9216,128]{1,0:T(8,128)} %bitcast.5, f32[2,4,72,8,128]{4,3,2,1,0:T(8,128)} %horiz_hbm.1, f32[2,2,72,8,128]{4,3,2,1,0:T(8,128)} %vert_hbm.1, f32[128,1152]{1,0:T(8,128)} %bitcast.7, ...), custom_call_target="tpu_custom_call" | custom-call | tf_op jit(solution)/shard_map/pallas_call | solution.py:584
  57.0 4.9 %broadcast_add_fusion = f32[16,72,8,128]{3,2,1,0:T(8,128)} fusion(f32[16,72,8,128]{3,2,1,0:T(8,128)} %bitcast.6, f32[72,8,128]{2,1,0:T(8,128)} %bitcast.8), kind=kLoop, calls=%fused_computation | loop fusion | flops 1179648 | bytes 9732096 | tf_op jit(solution)/shard_map/add | solution.py:635
where the time goes:
time: 62.2 us; the launch traced here: 62 us
  Pallas kernels  55.6 us (89%)
  other arithmetic  4.94 us (8%)
  local copies, waits for them, and re-layouts  1.42 us (2%)
    pallas_call x1, Pallas kernels, transport(): pl.pallas_call(functools.partial(kernel, (tracers, levels, lats, lons, n_...  55.6 us
    add x1, other arithmetic, transport(): out.reshape(adjoint_in.shape) + extra.reshape(levels, lats, lons)[None]  4.94 us
    unnamed x1, local copies, waits for them, and re-layouts  1.42 us

commit v1 on v0

--- a/solution.py
+++ b/solution.py
@@ -13,6 +13,7 @@
 GROUP = 4
 PITCH = 16
 BLOCK = 8
+VMEM_LIMIT = 33 * 1024 * 1024
 
 
 def log_of(value):
@@ -143,9 +144,9 @@
                 pole_matrix[step, p, lons : 2 * lons, :] = high
                 pole_matrix[step, p, 2 * lons : 3 * lons, :] = low
 
-    counts = jnp.broadcast_to(count_ref[...], (senders, senders)).T
-    slot = lax.broadcasted_iota(jnp.int32, (senders, slots), 1)
-    columns = jnp.where(slot < counts[:, :slots], col_ref[...], -1)
+    slot = lax.broadcasted_iota(jnp.int32, (slots, senders), 0)
+    filled = jnp.where(slot < count_ref[...], col_ref[...], -1)
+    columns = jnp.concatenate([filled] * (senders // slots), axis=0).T
     for j in range(slots):
         spread = jnp.broadcast_to(columns[:, j : j + 1], (senders, lons))
         for a in range(n_lat):
@@ -567,16 +568,21 @@
     extra_copy.wait()
 
 
+def stay(array):
+    return pltpu.with_memory_space_constraint(array, pltpu.HBM)
+
+
 def transport(mesh_shape, adjoint_in, horiz_frac, vert_frac, shift, frac, sound, cols, counts):
     tracers, levels, lats, lons = adjoint_in.shape
     n_lat, n_lon = mesh_shape
-    senders, slots = cols.shape
+    slots, senders = cols.shape
     groups = tracers // GROUP
     blocks = levels // BLOCK
     per_group = GROUP * levels
     features = sound.shape[1]
     f32 = jnp.float32
     any_spec = pl.BlockSpec(memory_space=pl.ANY)
+    hbm = pl.BlockSpec(memory_space=pltpu.HBM)
     vmem = pl.BlockSpec(memory_space=pltpu.VMEM)
     smem = pl.BlockSpec(memory_space=pltpu.SMEM)
     dma = pltpu.SemaphoreType.DMA
@@ -587,7 +593,7 @@
             jax.ShapeDtypeStruct((rows, lons), f32),
             jax.ShapeDtypeStruct((levels * lats, lons), f32),
         ),
-        in_specs=[smem, smem, any_spec, any_spec, any_spec, any_spec, vmem, vmem],
+        in_specs=[smem, smem, hbm, hbm, hbm, hbm, vmem, vmem],
         out_specs=(any_spec, any_spec),
         scratch_shapes=[
             pltpu.VMEM((rows + levels * lats, lons), f32),
@@ -629,9 +635,18 @@
             dma((STEPS, groups + 1, n_lon)),
         ],
         compiler_params=pltpu.CompilerParams(
-            collective_id=0, has_side_effects=True, vmem_limit_bytes=60 * 1024 * 1024
+            collective_id=0, has_side_effects=True, vmem_limit_bytes=VMEM_LIMIT
         ),
-    )(shift, frac, adjoint_in.reshape(rows, lons), horiz_frac, vert_frac, sound, cols, counts)
+    )(
+        stay(shift),
+        stay(frac),
+        stay(adjoint_in.reshape(rows, lons)),
+        stay(horiz_frac),
+        stay(vert_frac),
+        stay(sound),
+        stay(cols),
+        stay(counts),
+    )
     return out.reshape(adjoint_in.shape) + extra.reshape(levels, lats, lons)[None]
 
 
@@ -656,7 +671,7 @@
             polar_shift,
             polar_frac,
             sound_forcing[0],
-            sound_col[0],
+            sound_col[0].T,
             sound_count,
         )
 

time: 62.2 us -> 58.6 us (0.942)
  other arithmetic: 4.94 us -> 2.56 us
  local copies, waits for them, and re-layouts: 1.42 us -> 0 us
    add x1, other arithmetic: 4.94 us -> 2.56 us  [transport(): out.reshape(adjoint_in.shape) + extra.reshape(levels, lats, lons)[None]]
    unnamed x1 -> x0, local copies, waits for them, and re-layouts: 1.42 us -> none
where the time goes in v1:
time: 58.6 us; the launch traced here: 58.4 us
  Pallas kernels  55.9 us (95%)
  other arithmetic  2.56 us (4%)
    pallas_call x1, Pallas kernels, transport(): pl.pallas_call(functools.partial(kernel, (tracers, levels, lats, lons, n_...  55.9 us
    add x1, other arithmetic, transport(): out.reshape(adjoint_in.shape) + extra.reshape(levels, lats, lons)[None]  2.56 us

profile of v1, /device:TPU:0, one launch (start us, length us, event | category | flops | bytes accessed | tf_op | source)
XLA Modules:
  0.0 58.4 jit_solution(6784424107205693067)
XLA Ops:
  0.0 55.9 %shard_map.82 = (f32[9216,128]{1,0:T(8,128)S(1)}, f32[576,128]{1,0:T(8,128)S(1)}) custom-call(s32[2,4]{1,0:T(2,128)} %shift_ref.1, f32[2,4]{1,0:T(2,128)} %frac_ref.1, f32[9216,128]{1,0:T(8,128)} %bitcast.9, f32[2,4,72,8,128]{4,3,2,1,0:T(8,128)} %horiz_hbm.1, f32[2,2,72,8,128]{4,3,2,1,0:T(8,128)} %vert_hbm.1, f32[128,1152]{1,0:T(8,128)} %bitcast.10, ...), custom_call_target="tpu_custom_call" | custom-call | tf_op jit(solution)/shard_map/pallas_call | solution.py:590
  55.9 2.6 %broadcast_add_fusion = f32[16,72,8,128]{3,2,1,0:T(8,128)} fusion(f32[16,72,8,128]{3,2,1,0:T(8,128)S(1)} %bitcast.7, f32[72,8,128]{2,1,0:T(8,128)S(1)} %bitcast.8), kind=kLoop, calls=%fused_computation | loop fusion | flops 1179648 | bytes 9732096 | tf_op jit(solution)/shard_map/add | solution.py:650

commit v2 on v1

--- a/solution.py
+++ b/solution.py
@@ -100,16 +100,20 @@
     lane = lax.broadcasted_iota(jnp.int32, (lats, lons), 1)
     sub = lax.broadcasted_iota(jnp.int32, (lats, lons), 0)
 
-    volume = tracers * levels * lats
+    slab = GROUP * levels * lats
     load_vert = pltpu.make_async_copy(vert_hbm, vert, load_sem.at[0])
-    load_field = pltpu.make_async_copy(adjoint_hbm, field.at[pl.ds(0, volume)], load_sem.at[1])
-    load_horiz = pltpu.make_async_copy(horiz_hbm, horiz, load_sem.at[2])
+    load_horiz = pltpu.make_async_copy(horiz_hbm, horiz, load_sem.at[1])
     load_own = pltpu.make_async_copy(
-        sound_hbm.at[pl.ds(lat * n_lon, n_lon)], first_recv.at[lat], load_sem.at[3]
+        sound_hbm.at[pl.ds(lat * n_lon, n_lon)], first_recv.at[lat], load_sem.at[2]
     )
+
+    def load_slab(g):
+        rows = pl.ds(pl.multiple_of(g * slab, slab), slab)
+        return pltpu.make_async_copy(adjoint_hbm.at[rows], field.at[rows], load_sem.at[3 + g])
+
     load_vert.start()
-    load_field.start()
-    load_horiz.start()
+    for g in range(groups):
+        load_slab(g).start()
     load_own.start()
 
     barrier = pltpu.get_barrier_semaphore()
@@ -525,8 +529,6 @@
 
         lax.fori_loop(lo, hi, turn, 0)
 
-    slab = GROUP * levels * lats
-
     def out_copy(g):
         rows = pl.ds(pl.multiple_of(g * slab, slab), slab)
         return pltpu.make_async_copy(field.at[rows], out_hbm.at[rows], out_sem.at[g])
@@ -540,9 +542,13 @@
         main(g).end(0)
         out_copy(g).start()
 
+    def first(g):
+        load_slab(g).wait()
+        main(g).begin(1)
+
+    load_horiz.start()
     load_vert.wait()
-    load_field.wait()
-    over(0, groups, lambda g: main(g).begin(1))
+    over(0, groups, first)
     forward()
     load_horiz.wait()
     over(0, groups, middle)
@@ -621,7 +627,7 @@
             pltpu.VMEM((STEPS, n_lon, lats, lons), f32),
             pltpu.VMEM((NPOLE, levels, lons), f32),
             pltpu.VMEM((STEPS, NPOLE, 3 * lons, lons), jnp.bfloat16),
-            dma((4,)),
+            dma((3 + groups,)),
             dma((groups + 1,)),
             dma((n_lat,)),
             dma((n_lat,)),

time: 58.6 us -> 58.6 us (level)
  no operation moved by 1% of the time
where the time goes in v2:
time: 58.6 us; the launch traced here: 58.5 us
  Pallas kernels  55.9 us (95%)
  other arithmetic  2.56 us (4%)
    pallas_call x1, Pallas kernels, transport(): pl.pallas_call(functools.partial(kernel, (tracers, levels, lats, lons, n_...  55.9 us
    add x1, other arithmetic, transport(): out.reshape(adjoint_in.shape) + extra.reshape(levels, lats, lons)[None]  2.56 us

profile of v2, /device:TPU:0, one launch (start us, length us, event | category | flops | bytes accessed | tf_op | source)
XLA Modules:
  0.0 58.5 jit_solution(8731313506506154936)
XLA Ops:
  0.0 55.9 %shard_map.82 = (f32[9216,128]{1,0:T(8,128)S(1)}, f32[576,128]{1,0:T(8,128)S(1)}) custom-call(s32[2,4]{1,0:T(2,128)} %shift_ref.1, f32[2,4]{1,0:T(2,128)} %frac_ref.1, f32[9216,128]{1,0:T(8,128)} %bitcast.9, f32[2,4,72,8,128]{4,3,2,1,0:T(8,128)} %horiz_hbm.1, f32[2,2,72,8,128]{4,3,2,1,0:T(8,128)} %vert_hbm.1, f32[128,1152]{1,0:T(8,128)} %bitcast.10, ...), custom_call_target="tpu_custom_call" | custom-call | tf_op jit(solution)/shard_map/pallas_call | solution.py:596
  55.9 2.6 %broadcast_add_fusion = f32[16,72,8,128]{3,2,1,0:T(8,128)} fusion(f32[16,72,8,128]{3,2,1,0:T(8,128)S(1)} %bitcast.7, f32[72,8,128]{2,1,0:T(8,128)S(1)} %bitcast.8), kind=kLoop, calls=%fused_computation | loop fusion | flops 1179648 | bytes 9732096 | tf_op jit(solution)/shard_map/add | solution.py:656
